TPU v7x, 32 devices: a whole 2x2x4 slice. The times are simulated.
32 devices in a mesh: ctx: 4 (over z), dp: 4 (over y, x), section: 2 (over core).
Axes of the slice: x: 2, y: 2, z: 4, core: 2. Of those that a mesh axis runs over, the one named last changes fastest.
Arguments:
- tokens: bfloat16 [2, 4, 512, 4096], P('section', 'dp', 'ctx'), may hold values from -6 to 6
- norm_gain: float32 [2, 4096], P('section'), may hold values from 0.1 to 1.9
- query_weight: bfloat16 [2, 4096, 512], P('section', 'dp'), may hold values from -0.421875 to 0.421875
- key_weight: bfloat16 [2, 4096, 128], P('section', 'dp'), may hold values from -0.421875 to 0.421875
- value_weight: bfloat16 [2, 4096, 128], P('section', 'dp'), may hold values from -0.09375 to 0.09375
- block_order: int32 [2, 4, 8], P('section', 'dp'), may hold values from 0 to 7, each once within a row
- doc_ids: int32 [2, 4, 512], P('section', 'dp'), may hold values from 0 to 3, never falling along the last dimension, each value on 1 to 256 neighbouring positions
Outputs:
- passed: bfloat16 [2, 4, 512, 512], P('section', 'dp', 'ctx')
Inputs may be any that keep to these rules, and one draw needn't show every extreme that they name: `block_order`: each row is a permutation of the block numbers. `doc_ids`: never falling along positions; every document holds 1 to 256 positions, and one holds exactly 256.
All inputs are finite; a program needn't handle non-finite values.
Results may differ from a plain program's by a relative error of at most 0.012.
Values may be sent and summed in bfloat16 or wider, within the bound.
No kernel may reach another device: no remote copies, remote signals or barrier semaphores. Data moves between devices by JAX's collectives and lax.ppermute only.
A program may use at most 64 MiB of HBM per device.

v0:
```python
import jax
import jax.numpy as jnp
from jax import lax
from jax.sharding import PartitionSpec as P

ROPE_BASE = 500000.0
EPSILON = 1e-05
MASKED = -1e30


def passed_along(x, axis, by):
    length = lax.axis_size(axis)
    return lax.ppermute(x, axis, [(i, (i + by) % length) for i in range(length)])


def rotate_pairs(values, positions, head_size):
    count_rows = values.shape[0]
    shaped = values.reshape(count_rows, -1, head_size)
    halfway = head_size // 2
    freqs = ROPE_BASE ** (-jnp.arange(halfway, dtype=jnp.float32) * 2.0 / head_size)
    angles = positions.astype(jnp.float32)[:, None, None] * freqs[None, None, :]
    cosine = jnp.cos(angles)
    sine = jnp.sin(angles)
    first_half = shaped[..., :halfway]
    second_half = shaped[..., halfway:]
    turned = jnp.concatenate(
        [first_half * cosine - second_half * sine, second_half * cosine + first_half * sine],
        axis=-1,
    )
    return turned.reshape(count_rows, -1)


def local(tokens, norm_gain, query_weight, key_weight, value_weight, block_order, doc_ids):
    rows_here = tokens[0, 0]
    row_count = rows_here.shape[0]
    block_rows = doc_ids.shape[2] // block_order.shape[2]
    head_size = key_weight.shape[2]
    query_width = query_weight.shape[2]
    query_heads = query_width // head_size
    widened = rows_here.astype(jnp.float32)
    normed = (
        widened
        * lax.rsqrt(jnp.mean(widened * widened, axis=-1, keepdims=True) + EPSILON)
        * norm_gain[0][None, :]
    ).astype(jnp.bfloat16)
    spread = lax.all_to_all(normed, "dp", split_axis=1, concat_axis=0, tiled=True)
    joined = jnp.concatenate([query_weight[0], key_weight[0], value_weight[0]], axis=1)
    projected = lax.psum_scatter(
        jnp.dot(spread, joined, preferred_element_type=jnp.float32),
        "dp",
        scatter_dimension=0,
        tiled=True,
    )
    q_raw = projected[:, :query_width]
    k_raw = projected[:, query_width : query_width + head_size]
    v_raw = projected[:, query_width + head_size :]
    order = block_order[0, 0]
    within = jnp.arange(block_rows, dtype=jnp.int32)
    all_positions = (order[:, None] * block_rows + within[None, :]).reshape(-1)
    key_documents = jnp.take(doc_ids[0, 0], all_positions)
    cycle_index = lax.axis_index("ctx")
    query_positions = lax.dynamic_slice_in_dim(all_positions, cycle_index * row_count, row_count)
    query_documents = lax.dynamic_slice_in_dim(key_documents, cycle_index * row_count, row_count)
    queries = (
        rotate_pairs(q_raw, query_positions, head_size)
        .astype(jnp.bfloat16)
        .reshape(row_count, query_heads, head_size)
        .transpose(1, 0, 2)
    )
    keys = rotate_pairs(k_raw, query_positions, head_size).astype(jnp.bfloat16)
    values = v_raw.astype(jnp.bfloat16)
    scaling = head_size ** (-0.5)

    def absorb(state, key_block, value_block, key_pos, key_doc):
        run_max, run_total, run_acc = state
        scores = (
            jnp.einsum("hqd,kd->hqk", queries, key_block, preferred_element_type=jnp.float32)
            * scaling
        )
        allowed = (key_doc[None, :] == query_documents[:, None]) & (
            key_pos[None, :] <= query_positions[:, None]
        )
        scores = jnp.where(allowed[None], scores, MASKED)
        new_max = jnp.maximum(run_max, jnp.max(scores, axis=-1))
        weights = jnp.where(allowed[None], jnp.exp(scores - new_max[..., None]), 0.0)
        factor = jnp.exp(run_max - new_max)
        new_total = run_total * factor + jnp.sum(weights, axis=-1)
        new_acc = run_acc * factor[..., None] + jnp.einsum(
            "hqk,kd->hqd",
            weights.astype(jnp.bfloat16),
            value_block,
            preferred_element_type=jnp.float32,
        )
        return (new_max, new_total, new_acc)

    def attend(state, pieces):
        key_piece, value_piece = pieces
        piece_rows = key_piece.shape[0]
        if piece_rows > 1024 and piece_rows % 1024 == 0:
            groups = piece_rows // 1024

            def inner(inner_state, stacked):
                return (absorb(inner_state, stacked[0], stacked[1], stacked[2], stacked[3]), None)

            stacked_all = (
                key_piece.reshape(groups, 1024, -1),
                value_piece.reshape(groups, 1024, -1),
                all_positions.reshape(groups, 1024),
                key_documents.reshape(groups, 1024),
            )
            result, unused = lax.scan(inner, state, stacked_all)
            return result
        return absorb(state, key_piece, value_piece, all_positions, key_documents)

    starting_state = (
        jnp.full((query_heads, row_count), MASKED, jnp.float32),
        jnp.zeros((query_heads, row_count), jnp.float32),
        jnp.zeros((query_heads, row_count, head_size), jnp.float32),
    )
    final_max, final_total, final_acc = attend(
        starting_state,
        (
            lax.all_gather(keys, "ctx", axis=0, tiled=True),
            lax.all_gather(values, "ctx", axis=0, tiled=True),
        ),
    )
    attended = (
        (final_acc / final_total[..., None])
        .transpose(1, 0, 2)
        .reshape(row_count, query_width)
        .astype(jnp.bfloat16)
    )
    passed = passed_along(attended, "section", 1)
    return passed[None, None]


def solution(mesh):
    in_specs = (
        P("section", "dp", "ctx", None),
        P("section", None),
        P("section", "dp", None),
        P("section", "dp", None),
        P("section", "dp", None),
        P("section", "dp", None),
        P("section", "dp", None),
    )
    out_specs = P("section", "dp", "ctx", None)
    return jax.shard_map(local, mesh=mesh, in_specs=in_specs, out_specs=out_specs, check_vma=False)
```

profile of v0, /device:TPU:0, one launch (start us, length us, event | category | flops | bytes accessed | tf_op | source)
XLA Modules:
  0.0 104.1 jit_solution(5740808734382966192)
XLA Ops:
  6.5 0.0 copy-start
  6.5 0.0 reduce-scatter.2.cloned.1.call-start
  6.5 0.5 broadcast.241
  7.1 1.4 %reduce.4 = f32[4096]{0:T(1024)S(1)} reduce(f32[1,4096]{1,0:T(1,128)} %param.8, f32[]{:T(128)} %broadcast.241), dimensions={0}, to_apply=%param.8.reduce_sub_computation.3 | reduce | bytes 32772 | tf_op args[1]
  8.5 1.6 %copy.22 = bf16[1,1,128,4096]{2,3,1,0:T(8,128)(2,1)S(1)} copy(bf16[1,1,128,4096]{3,2,1,0:T(8,128)(2,1)} %param.7) | data formatting | bytes 2097152 | tf_op args[0]
  10.1 0.6 multiply_reduce_fusion
  10.7 0.7 multiply_convert_fusion
  11.4 19.1 %all_to_all.16 = bf16[128,4,1024]{0,2,1:T(8,128)(2,1)S(1)} all-to-all(bf16[128,4,1024]{0,2,1:T(8,128)(2,1)S(1)} %multiply_convert_fusion), channel_id=1, replica_groups=mesh['ctx'=4,'dp'=4,'section'=2] {'dp'}, dimensions={1} | all-to-all | bytes 2097152 | tf_op jit(solution)/shard_map/all_to_all | solution.py:46
  30.5 0.0 copy-start.1
  30.5 0.0 copy-start.2
  30.5 0.5 copy.23
  31.0 0.7 copy-done.1
  31.7 0.0 copy-done.2
  31.8 3.1 %fusion = f32[512,768]{0,1:T(8,128)} fusion(bf16[512,1024]{1,0:T(8,128)(2,1)S(1)} %bitcast.49, bf16[1024,128]{1,0:T(8,128)(2,1)S(1)} %bitcast.55, bf16[1024,128]{1,0:T(8,128)(2,1)} %bitcast.56, bf16[1024,512]{1,0:T(8,128)(2,1)S(1)} %bitcast.54), kind=kOutput, calls=%fused_computation.3 | convolution fusion | flops 810024960 | bytes 4194304 | tf_op jit(solution)/shard_map/dot_general | solution.py:49
  34.9 0.0 copy-start.3
  34.9 0.0 reduce-scatter.2.cloned.1.call-update
  34.9 0.6 copy-done.3
  35.6 0.1 iota_add_fusion
  35.6 0.1 add.99
  35.7 0.1 add.102
  35.8 0.0 copy-done
  35.8 3.5 %gather_fusion = s32[512]{0:T(512)S(1)} fusion(s32[512]{0:T(512)S(1)} %bitcast.46, s32[1024]{0:T(1024)S(1)} %pad_clamp_fusion), kind=kCustom, calls=%fused_computation | custom fusion | bytes 6144 | tf_op jit(solution)/shard_map/jit(_take)/gather | solution.py:60
  39.3 0.1 dynamic_slice.6
  39.4 0.1 fusion.31
  39.5 0.1 compare_and_fusion
  39.6 0.3 multiply_cosine_fusion
  40.0 26.0 %reduce-scatter.2.cloned.1.call-done = f32[128,768]{0,1:T(8,128)} async-done(((f32[512,768]{0,1:T(8,128)}), f32[128,768]{0,1:T(8,128)}) %reduce-scatter.2.cloned.1.call-update) | async-done | bytes 393232 | tf_op jit(solution)/shard_map/reduce_scatter | solution.py:48
  65.9 0.8 slice_bitcast_fusion
  66.8 0.2 fusion.25
  67.0 12.3 %all-gather = bf16[512,1,128]{0,2,1:T(8,128)(2,1)S(1)} all-gather(bf16[128,1,128]{0,2,1:T(8,128)(2,1)S(1)} %pad_maximum_fusion), channel_id=2, replica_groups=mesh['ctx'=4,'dp'=4,'section'=2] {'ctx'}, dimensions={0}, use_global_device_ids=true | all-gather | bytes 163840 | tf_op jit(solution)/shard_map/all_gather | solution.py:123
  79.3 1.0 slice.31
  80.3 0.1 copy.33
  80.4 0.1 copy.32
  80.6 0.1 subtract_convert_fusion
  80.7 0.5 fusion.33
  81.1 0.9 slice.44
  82.0 12.2 %all_gather.7 = bf16[512,128]{0,1:T(8,128)(2,1)S(1)} all-gather(bf16[128,128]{0,1:T(8,128)(2,1)S(1)} %slice.44), channel_id=1, replica_groups=mesh['ctx'=4,'dp'=4,'section'=2] {'ctx'}, dimensions={0}, use_global_device_ids=true | all-gather | bytes 163840 | tf_op jit(solution)/shard_map/all_gather | solution.py:124
  94.2 0.3 fusion.10
  94.6 0.5 fusion.9
  95.1 0.1 copy.28
  95.2 0.1 collective-permute-start
  95.3 1.3 %collective-permute-done = bf16[128,512]{1,0:T(8,128)(2,1)S(1)} collective-permute-done((bf16[128,512]{1,0:T(8,128)(2,1)S(1)}, bf16[128,512]{1,0:T(8,128)(2,1)S(1)}, u32[]{:S(2)}, u32[]{:S(2)}) %collective-permute-start) | collective-permute-done | bytes 131104 | tf_op jit(solution)/shard_map/ppermute | solution.py:13
  96.6 0.7 copy.35
  (11 shorter events, 0.1 us)
Async XLA Ops:
  6.5 29.3 %copy-start = (s32[1,1,512]{2,1,0:T(1,128)S(1)}, s32[1,1,512]{2,1,0:T(1,128)}, u32[]{:S(2)}) copy-start(s32[1,1,512]{2,1,0:T(1,128)} %param.13) | copy-start | bytes 6148
  6.5 59.4 %reduce-scatter.2.cloned.1.call-start = ((), (), s32[]{:S(2)}) async-start(), calls=%async_computation.2 | async-start | bytes 1966080 | tf_op jit(solution)/shard_map/reduce_scatter | solution.py:48
  30.5 1.2 %copy-start.1 = (bf16[1,1024,512]{2,1,0:T(8,128)(2,1)S(1)}, bf16[1,1024,512]{2,1,0:T(8,128)(2,1)}, u32[]{:S(2)}) copy-start(bf16[1,1024,512]{2,1,0:T(8,128)(2,1)} %param.9) | copy-start | bytes 3145732
  30.5 1.3 %copy-start.2 = (bf16[1,1024,128]{2,1,0:T(8,128)(2,1)S(1)}, bf16[1,1024,128]{2,1,0:T(8,128)(2,1)}, u32[]{:S(2)}) copy-start(bf16[1,1024,128]{2,1,0:T(8,128)(2,1)} %param.11) | copy-start | bytes 786436
  34.9 0.7 copy-start.3
  95.2 1.4 %collective-permute-start = (bf16[128,512]{1,0:T(8,128)(2,1)S(1)}, bf16[128,512]{1,0:T(8,128)(2,1)S(1)}, u32[]{:S(2)}, u32[]{:S(2)}) collective-permute-start(bf16[128,512]{1,0:T(8,128)(2,1)S(1)} %copy.28), channel_id=1, source_target_pairs={{0,1},{1,0},{2,3},{3,2},{4,5},{5,4},{6,7},{7,6},{8,9},{9,8},{10,11... | collective-permute-start | bytes 393224 | tf_op jit(solution)/shard_map/ppermute | solution.py:13
Sparse Core Ops, SparseCore 0:
  35.0 30.8 reduce-scatter.1
where the time goes:
time: 105 us; the launch traced here: 104 us
  blocking collectives  43.7 us (42%)
  waiting for transfers between devices  27.3 us (26%)
  between operations  13.5 us (13%)
  local copies, waits for them, and re-layouts  11.5 us (11%)
  matrix products  4.04 us (4%)
  other arithmetic  3.93 us (4%)
    reduce_scatter x1, waiting for transfers between devices, local(): lax.psum_scatter(jnp.dot(spread, joined, preferred_element_type=jnp.float...  26 us
    all_to_all x1, blocking collectives, local(): lax.all_to_all(normed, 'dp', split_axis=1, concat_axis=0, tiled=True)  19.1 us
    all_gather x1, blocking collectives, local(): lax.all_gather(keys, 'ctx', axis=0, tiled=True)  12.3 us
    all_gather x1, blocking collectives, local(): lax.all_gather(values, 'ctx', axis=0, tiled=True)  12.2 us
    unnamed x13, local copies, waits for them, and re-layouts  4.4 us
    gather x1, local copies, waits for them, and re-layouts, local(): key_documents = jnp.take(doc_ids[0, 0], all_positions)  3.51 us
    dot_general x1, matrix products, local(): jnp.dot(spread, joined, preferred_element_type=jnp.float32)  3.13 us
  transfers between devices with their start and end apart: 2, of which 2 were waited for; matrix products, arithmetic and copies ran while one was open for 4% of the time, Pallas kernels for 0%

commit v1 on v0

--- a/solution.py
+++ b/solution.py
@@ -6,6 +6,11 @@
 ROPE_BASE = 500000.0
 EPSILON = 1e-05
 MASKED = -1e30
+
+
+def tiled_gather(array, axis, dim):
+    copies = jnp.concatenate([array] * lax.axis_size(axis), axis=dim)
+    return lax.all_to_all(copies, axis, dim, dim, tiled=True)
 
 
 def passed_along(x, axis, by):
@@ -119,10 +124,7 @@
     )
     final_max, final_total, final_acc = attend(
         starting_state,
-        (
-            lax.all_gather(keys, "ctx", axis=0, tiled=True),
-            lax.all_gather(values, "ctx", axis=0, tiled=True),
-        ),
+        (lax.all_gather(keys, "ctx", axis=0, tiled=True), tiled_gather(values, "ctx", 0)),
     )
     attended = (
         (final_acc / final_total[..., None])

time: 105 us -> 97.3 us (0.927)
  blocking collectives: 43.7 us -> 32 us
  starting transfers between devices: 0.07 us -> 4.66 us
    all_gather x1 -> x0, blocking collectives: 12.2 us -> none  [local(): lax.all_gather(values, 'ctx', axis=0, tiled=True)]
    all_to_all x0 -> x1, starting transfers between devices: none -> 4.59 us  [tiled_gather(): return lax.all_to_all(copies, axis, dim, dim, tiled=True)]
  transfers between devices with their start and end apart: 2 -> 3, of which waited for: 2 -> 2; matrix products, arithmetic and copies ran while one was open for 4% -> 7% of each run, Pallas kernels for 0% -> 0%
where the time goes in v1:
time: 97.3 us; the launch traced here: 96.9 us
  blocking collectives  32 us (33%)
  waiting for transfers between devices  27.3 us (28%)
  between operations  13.6 us (14%)
  local copies, waits for them, and re-layouts  10.7 us (11%)
  starting transfers between devices  4.66 us (5%)
  other arithmetic  4.61 us (5%)
  matrix products  4.04 us (4%)
    reduce_scatter x1, waiting for transfers between devices, local(): lax.psum_scatter(jnp.dot(spread, joined, preferred_element_type=jnp.float...  26 us
    all_to_all x1, blocking collectives, local(): lax.all_to_all(normed, 'dp', split_axis=1, concat_axis=0, tiled=True)  19.1 us
    all_gather x1, blocking collectives, local(): lax.all_gather(keys, 'ctx', axis=0, tiled=True)  12.8 us
    all_to_all x1, starting transfers between devices, tiled_gather(): return lax.all_to_all(copies, axis, dim, dim, tiled=True)  4.59 us
    unnamed x13, local copies, waits for them, and re-layouts  4.4 us
    gather x1, local copies, waits for them, and re-layouts, local(): key_documents = jnp.take(doc_ids[0, 0], all_positions)  3.51 us
    dot_general x1, matrix products, local(): jnp.dot(spread, joined, preferred_element_type=jnp.float32)  3.14 us
  transfers between devices with their start and end apart: 3, of which 2 were waited for; matrix products, arithmetic and copies ran while one was open for 7% of the time, Pallas kernels for 0%

profile of v1, /device:TPU:0, one launch (start us, length us, event | category | flops | bytes accessed | tf_op | source)
XLA Modules:
  0.0 96.9 jit_solution(7422109725364633413)
XLA Ops:
  6.5 0.0 copy-start
  6.5 0.0 reduce-scatter.2.cloned.1.call-start
  6.5 0.5 broadcast.241
  7.1 1.4 %reduce.4 = f32[4096]{0:T(1024)S(1)} reduce(f32[1,4096]{1,0:T(1,128)} %param.8, f32[]{:T(128)} %broadcast.241), dimensions={0}, to_apply=%param.8.reduce_sub_computation.3 | reduce | bytes 32772 | tf_op args[1]
  8.5 1.6 %copy.29 = bf16[1,1,128,4096]{2,3,1,0:T(8,128)(2,1)S(1)} copy(bf16[1,1,128,4096]{3,2,1,0:T(8,128)(2,1)} %param.7) | data formatting | bytes 2097152 | tf_op args[0]
  10.1 0.6 multiply_reduce_fusion
  10.7 0.7 multiply_convert_fusion
  11.4 19.1 %all_to_all.28 = bf16[128,4,1024]{0,2,1:T(8,128)(2,1)S(1)} all-to-all(bf16[128,4,1024]{0,2,1:T(8,128)(2,1)S(1)} %multiply_convert_fusion), channel_id=1, replica_groups=mesh['ctx'=4,'dp'=4,'section'=2] {'dp'}, dimensions={1} | all-to-all | bytes 2097152 | tf_op jit(solution)/shard_map/all_to_all | solution.py:51
  30.5 0.0 copy-start.1
  30.5 0.0 copy-start.2
  30.5 0.5 copy.30
  31.0 0.7 copy-done.1
  31.7 0.0 copy-done.2
  31.8 3.1 %fusion = f32[512,768]{0,1:T(8,128)} fusion(bf16[512,1024]{1,0:T(8,128)(2,1)S(1)} %bitcast.54, bf16[1024,128]{1,0:T(8,128)(2,1)S(1)} %bitcast.60, bf16[1024,128]{1,0:T(8,128)(2,1)} %bitcast.61, bf16[1024,512]{1,0:T(8,128)(2,1)S(1)} %bitcast.59), kind=kOutput, calls=%fused_computation.3 | convolution fusion | flops 810024960 | bytes 4194304 | tf_op jit(solution)/shard_map/dot_general | solution.py:54
  34.9 0.0 copy-start.3
  34.9 0.0 reduce-scatter.2.cloned.1.call-update
  34.9 0.6 copy-done.3
  35.6 0.1 iota_add_fusion
  35.6 0.1 add.99
  35.7 0.1 add.102
  35.8 0.0 copy-done
  35.8 3.5 %gather_fusion = s32[512]{0:T(512)S(1)} fusion(s32[512]{0:T(512)S(1)} %bitcast.51, s32[1024]{0:T(1024)S(1)} %pad_clamp_fusion), kind=kCustom, calls=%fused_computation | custom fusion | bytes 6144 | tf_op jit(solution)/shard_map/jit(_take)/gather | solution.py:65
  39.4 0.1 dynamic_slice.6
  39.4 0.1 fusion.30
  39.5 0.1 compare_and_fusion
  39.7 0.3 multiply_cosine_fusion
  40.0 26.0 %reduce-scatter.2.cloned.1.call-done = f32[128,768]{0,1:T(8,128)} async-done(((f32[512,768]{0,1:T(8,128)}), f32[128,768]{0,1:T(8,128)}) %reduce-scatter.2.cloned.1.call-update) | async-done | bytes 393232 | tf_op jit(solution)/shard_map/reduce_scatter | solution.py:53
  65.9 0.0 slice-start
  65.9 0.9 slice.44
  66.8 0.7 copy_bitcast_fusion
  67.5 4.6 %all-to-all-start.1 = ((bf16[4,128,128]{1,2,0:T(8,128)(2,1)}), bf16[4,128,128]{1,2,0:T(8,128)(2,1)S(1)}, u32[]{:S(2)}, u32[]{:S(2)}) async-start(bf16[4,128,128]{1,2,0:T(8,128)(2,1)} %copy_bitcast_fusion), calls=%async_computation.2 | async-start | bytes 262144 | tf_op jit(solution)/shard_map/all_to_all | solution.py:13
  72.1 0.8 slice_bitcast_fusion
  72.9 0.2 fusion.24
  73.2 12.8 %all-gather = bf16[512,1,128]{0,2,1:T(8,128)(2,1)S(1)} all-gather(bf16[128,1,128]{0,2,1:T(8,128)(2,1)S(1)} %pad_maximum_fusion), channel_id=2, replica_groups=mesh['ctx'=4,'dp'=4,'section'=2] {'ctx'}, dimensions={0}, use_global_device_ids=true | all-gather | bytes 163840 | tf_op jit(solution)/shard_map/all_gather | solution.py:127
  86.0 0.0 slice-done
  86.0 0.1 copy.42
  86.1 0.1 copy.41
  86.3 0.1 subtract_convert_fusion
  86.4 0.5 fusion.32
  86.8 0.4 fusion.10
  87.2 0.0 all-to-all-done.1
  87.2 0.1 copy.36
  87.3 0.1 reshape.301
  87.4 0.5 fusion.9
  87.8 0.1 copy.37
  88.0 0.1 collective-permute-start
  88.0 1.3 %collective-permute-done = bf16[128,512]{1,0:T(8,128)(2,1)S(1)} collective-permute-done((bf16[128,512]{1,0:T(8,128)(2,1)S(1)}, bf16[128,512]{1,0:T(8,128)(2,1)S(1)}, u32[]{:S(2)}, u32[]{:S(2)}) %collective-permute-start) | collective-permute-done | bytes 131104 | tf_op jit(solution)/shard_map/ppermute | solution.py:18
  89.4 0.7 copy.46
  (11 shorter events, 0.1 us)
Async XLA Ops:
  6.5 29.3 %copy-start = (s32[1,1,512]{2,1,0:T(1,128)S(1)}, s32[1,1,512]{2,1,0:T(1,128)}, u32[]{:S(2)}) copy-start(s32[1,1,512]{2,1,0:T(1,128)} %param.13) | copy-start | bytes 6148
  6.5 59.4 %reduce-scatter.2.cloned.1.call-start = ((), (), s32[]{:S(2)}) async-start(), calls=%async_computation.3 | async-start | bytes 1966080 | tf_op jit(solution)/shard_map/reduce_scatter | solution.py:53
  30.5 1.2 %copy-start.1 = (bf16[1,1024,512]{2,1,0:T(8,128)(2,1)S(1)}, bf16[1,1024,512]{2,1,0:T(8,128)(2,1)}, u32[]{:S(2)}) copy-start(bf16[1,1024,512]{2,1,0:T(8,128)(2,1)} %param.9) | copy-start | bytes 3145732
  30.5 1.3 %copy-start.2 = (bf16[1,1024,128]{2,1,0:T(8,128)(2,1)S(1)}, bf16[1,1024,128]{2,1,0:T(8,128)(2,1)}, u32[]{:S(2)}) copy-start(bf16[1,1024,128]{2,1,0:T(8,128)(2,1)} %param.11) | copy-start | bytes 786436
  34.9 0.7 copy-start.3
  65.9 20.0 %slice-start = ((f32[128,768]{0,1:T(8,128)}), f32[128,512]{0,1:T(8,128)S(1)}, s32[]{:S(2)}) async-start(f32[128,768]{0,1:T(8,128)} %reduce-scatter.2.cloned.1.call-done), calls=%async_computation.4 | async-start | bytes 524288 | tf_op jit(solution)/shard_map/slice | solution.py:59
  67.5 19.7 %all-to-all-start.1 = ((bf16[4,128,128]{1,2,0:T(8,128)(2,1)}), bf16[4,128,128]{1,2,0:T(8,128)(2,1)S(1)}, u32[]{:S(2)}, u32[]{:S(2)}) async-start(bf16[4,128,128]{1,2,0:T(8,128)(2,1)} %copy_bitcast_fusion), calls=%async_computation.2 | async-start | bytes 262144 | tf_op jit(solution)/shard_map/all_to_all | solution.py:13
  88.0 1.4 %collective-permute-start = (bf16[128,512]{1,0:T(8,128)(2,1)S(1)}, bf16[128,512]{1,0:T(8,128)(2,1)S(1)}, u32[]{:S(2)}, u32[]{:S(2)}) collective-permute-start(bf16[128,512]{1,0:T(8,128)(2,1)S(1)} %copy.37), channel_id=1, source_target_pairs={{0,1},{1,0},{2,3},{3,2},{4,5},{5,4},{6,7},{7,6},{8,9},{9,8},{10,11... | collective-permute-start | bytes 393224 | tf_op jit(solution)/shard_map/ppermute | solution.py:18
Sparse Core Ops, SparseCore 0:
  35.1 30.8 reduce-scatter.1
